TPU v7x, 32 devices: a whole 2x2x4 slice. The times are simulated.
32 devices in a mesh: segment: 8 (over z, x), tp: 4 (over y, core).
Axes of the slice: x: 2, y: 2, z: 4, core: 2. Of those that a mesh axis runs over, the one named last changes fastest.
Arguments:
- layer_inputs: bfloat16 [8, 2, 128, 2048], P('segment', None, 'tp'), may hold values from -100 to 100, as said below
- cotangent: bfloat16 [2, 2, 128, 2048], P(None, None, 'tp'), may hold values from -6 to 6
- gate_weight: bfloat16 [8, 2048, 4096], P('segment', None, 'tp'), may hold values from -1 to 1, as said below
- up_weight: bfloat16 [8, 2048, 4096], P('segment', None, 'tp'), may hold values from -1 to 1, as said below
- down_weight: bfloat16 [8, 4096, 2048], P('segment', 'tp'), may hold values from -1 to 1, as said below
- gate_momentum: float32 [8, 1024, 4096], P('segment', None, 'tp'), may hold values from -48 to 48
- up_momentum: float32 [8, 1024, 4096], P('segment', None, 'tp'), may hold values from -48 to 48
- down_momentum: float32 [8, 4096, 1024], P('segment', 'tp'), may hold values from -48 to 48
Outputs:
- input_gradient: bfloat16 [8, 2, 128, 2048], P('segment', None, 'tp')
- new_gate_momentum: float32 [8, 1024, 4096], P('segment', None, 'tp')
- new_up_momentum: float32 [8, 1024, 4096], P('segment', None, 'tp')
- new_down_momentum: float32 [8, 4096, 1024], P('segment', 'tp')
Inputs may be any that keep to these rules, and one draw needn't show every extreme that they name: `layer_inputs`: stored layer inputs, independent for every section and micro-batch. `gate_weight`: sections 2l and 2l + 1 hold equal copies of one layer's weights. `up_weight`: sections 2l and 2l + 1 hold equal copies of one layer's weights. `down_weight`: sections 2l and 2l + 1 hold equal copies of one layer's weights.
All inputs are finite; a program needn't handle non-finite values.
Results may differ from a plain program's by a relative error of at most 0.02.
Values may be sent and summed in bfloat16 or wider, within the bound.
A program may use at most 128 MiB of HBM per device.

v0:
```python
import functools
import jax
import jax.numpy as jnp
from jax import lax
from jax.experimental import pallas as pl
from jax.experimental.pallas import tpu as pltpu
from jax.sharding import PartitionSpec as P

epsilon = 1e-05
momentum_decay = 0.9


def passed_along(block, axis, distance):
    devices = range(lax.axis_size(axis))
    route = [(i - distance, i) for i in devices if i - distance in devices]
    return lax.ppermute(block, axis, route)


def partner(block, axis, distance):
    count = lax.axis_size(axis)
    route = []
    for low in range(count):
        high = low | 1 << distance
        if high != low and high < count:
            route += [(low, high), (high, low)]
    return lax.ppermute(block, axis, route)


def contract_last(left, right):
    return lax.dot_general(
        left, right, (((1,), (1,)), ((), ())), preferred_element_type=jnp.float32
    )


def contract_rows(left, right):
    return lax.dot_general(
        left, right, (((0,), (0,)), ((), ())), preferred_element_type=jnp.float32
    )


def rounded(values):
    return lax.optimization_barrier(values.astype(jnp.bfloat16)).astype(jnp.float32)


def project(rows, gate_w, up_w):
    gate = jnp.dot(rows, gate_w, preferred_element_type=jnp.float32)
    up = jnp.dot(rows, up_w, preferred_element_type=jnp.float32)
    return (gate, up)


def backward_factors(incoming_rows, gate, up, down_w):
    hidden_grad = contract_last(incoming_rows, down_w)
    sigma = jax.nn.sigmoid(gate)
    silu = gate * sigma
    hidden = (silu * up).astype(jnp.bfloat16)
    gate_grad = (hidden_grad * up * sigma * (1.0 + gate * (1.0 - sigma))).astype(jnp.bfloat16)
    up_grad = (hidden_grad * silu).astype(jnp.bfloat16)
    return (hidden, gate_grad, up_grad)


def owned(array, start, size, axis):
    return lax.dynamic_slice_in_dim(array, start, size, axis)


def shards(
    layer_inputs,
    cotangent,
    gate_weight,
    up_weight,
    down_weight,
    gate_momentum,
    up_momentum,
    down_momentum,
):
    segments = lax.axis_size("segment")
    depth = segments // 2
    segment = lax.axis_index("segment")
    direction = segment % 2
    lower = direction == 0
    position = segment // 2
    gate_w = gate_weight[0]
    up_w = up_weight[0]
    down_w = down_weight[0]
    inputs = layer_inputs[0].astype(jnp.float32)
    micro, rows_dev, width = inputs.shape
    half = width // 2
    hidden_dev = gate_w.shape[1]
    total_rows = rows_dev * lax.axis_size("tp")
    inverse_norm = lax.rsqrt(jnp.mean(inputs * inputs, axis=-1, keepdims=True) + epsilon)
    exact = inputs * inverse_norm
    normed = exact.astype(jnp.bfloat16)
    entry = lax.dynamic_index_in_dim(cotangent, direction, 0, keepdims=False)
    ticks = depth + micro - 1
    wide_store = jnp.zeros((micro, total_rows, width), jnp.bfloat16)
    narrow_store = jnp.zeros((micro, total_rows, hidden_dev), jnp.bfloat16)
    extra = (wide_store, narrow_store, narrow_store, narrow_store) + (wide_store,)

    def process(tick, received, state):
        outgoing, backs, extra = state
        index = tick - position
        active = (index >= 0) & (index < micro)
        slot = jnp.clip(index, 0, micro - 1)
        local_in = jnp.where(position == 0, entry[slot], received)
        incoming_rows = lax.all_gather(local_in, "tp", axis=0, tiled=True)
        full_rows = lax.all_gather(normed[slot], "tp", axis=0, tiled=True)

        def factors():
            gate, up = project(full_rows, gate_w, up_w)
            return backward_factors(incoming_rows, gate, up, down_w)

        def resting():
            blank = jnp.zeros((total_rows, hidden_dev), jnp.bfloat16)
            return (blank, blank, blank)

        hidden, gate_grad, up_grad = lax.cond(active, factors, resting)
        count = lax.axis_size("tp") * rows_dev

        def compute():
            return contract_last(gate_grad, gate_w) + contract_last(up_grad, up_w)

        def quiet():
            return jnp.zeros((count, width), jnp.float32)

        normed_grad = lax.psum_scatter(
            lax.cond(active, compute, quiet).astype(jnp.bfloat16),
            "tp",
            scatter_dimension=0,
            tiled=True,
        ).astype(jnp.float32)
        scale = inverse_norm[slot]
        base = exact[slot]
        back = local_in.astype(jnp.float32) + scale * (
            normed_grad - base * jnp.mean(normed_grad * base, axis=-1, keepdims=True)
        )
        back = back.astype(jnp.bfloat16)
        backs = lax.dynamic_update_index_in_dim(
            backs, jnp.where(active, back, backs[slot]), slot, 0
        )
        fresh = (incoming_rows, hidden, gate_grad, up_grad) + (full_rows,)
        extra = tuple(
            (
                lax.dynamic_update_index_in_dim(
                    store, jnp.where(active, item, store[slot]), slot, 0
                )
                for store, item in zip(extra, fresh)
            )
        )
        return (back, backs, extra)

    zero_rows = jnp.zeros((rows_dev, width), jnp.bfloat16)
    state = process(
        0, zero_rows, (zero_rows, jnp.zeros((micro, rows_dev, width), jnp.bfloat16), extra)
    )

    def advance(tick, state):
        received = passed_along(state[0], "segment", 2)
        return process(tick, received, state)

    outgoing, backs, extra = lax.fori_loop(1, ticks, advance, state)
    keep_start = jnp.where(lower, 0, half)
    send_start = half - keep_start
    flat_rows = micro * total_rows
    normed_all = extra[4]
    normed_flat = normed_all.reshape(flat_rows, width)
    incoming_flat = extra[0].reshape(flat_rows, width)
    hidden_flat = extra[1].reshape(flat_rows, hidden_dev)
    gate_flat = extra[2].reshape(flat_rows, hidden_dev)
    up_flat = extra[3].reshape(flat_rows, hidden_dev)
    arrived = partner(
        (
            owned(normed_flat, send_start, half, 1),
            owned(incoming_flat, send_start, half, 1),
            hidden_flat,
            gate_flat,
            up_flat,
        ),
        "segment",
        0,
    )
    normed_keep = owned(normed_flat, keep_start, half, 1)
    incoming_keep = owned(incoming_flat, keep_start, half, 1)
    gate_share = contract_rows(normed_keep, gate_flat) + rounded(
        contract_rows(arrived[0], arrived[3])
    )
    up_share = contract_rows(normed_keep, up_flat) + rounded(contract_rows(arrived[0], arrived[4]))
    down_share = contract_rows(hidden_flat, incoming_keep) + rounded(
        contract_rows(arrived[2], arrived[1])
    )
    new_gate = (momentum_decay * gate_momentum[0] + gate_share)[None]
    new_up = (momentum_decay * up_momentum[0] + up_share)[None]
    new_down = (momentum_decay * down_momentum[0] + down_share)[None]
    return (backs[None], new_gate, new_up, new_down)


def masks_even(count):
    return sorted(range(2, count, 2), key=lambda m: -(m & -m))


def relay_kernel(
    n,
    depth,
    li_ref,
    cot_ref,
    gate_hbm,
    up_hbm,
    down_hbm,
    back_ref,
    normed_out,
    incoming_out,
    hidden_out,
    gate_out,
    up_out,
    gate_w,
    up_w,
    down_w,
    nrm,
    inc,
    slope,
    silu_s,
    exact_s,
    inv_s,
    parts,
    rs_recv,
    z_send,
    gate_t,
    up_t,
    down_t,
    load_sem,
    ssem,
    rsem,
):
    micro, rows, width = li_ref.shape
    hid = down_w.shape[0]
    total = n * rows
    half = width // 2
    bits = n.bit_length() - 1
    pieces = ssem.shape[1]
    size = rows // pieces
    s = lax.axis_index("segment")
    t = lax.axis_index("tp")
    p = lax.div(s, 2)
    d = lax.rem(s, 2)
    mirror = s + 1 - 2 * d

    def flip(mask):
        value = t
        for b in range(bits):
            if mask >> b & 1:
                value = value + (1 << b) * (1 - 2 * lax.rem(lax.div(t, 1 << b), 2))
        return value

    def piece(c):
        return pl.ds(c * size, size)

    def copy(k, c, kind, slot, src, dst, device):
        return pltpu.make_async_remote_copy(
            src_ref=src,
            dst_ref=dst,
            send_sem=ssem.at[k, c, kind * n + slot],
            recv_sem=rsem.at[k, c, kind * n + slot],
            device_id=device,
            device_id_type=pl.DeviceIdType.MESH,
        )

    loads = [
        pltpu.make_async_copy(a, b, load_sem.at[i])
        for i, (a, b) in enumerate(((gate_hbm, gate_w), (up_hbm, up_w), (down_hbm, down_w)))
    ]
    for load in loads:
        load.start()

    barrier = pltpu.get_barrier_semaphore()

    def greet(device):
        pl.semaphore_signal(
            barrier, inc=1, device_id=device, device_id_type=pl.DeviceIdType.MESH
        )

    for b in range(bits):
        greet({"tp": flip(1 << b)})
    greet({"segment": mirror})

    @pl.when(p > 0)
    def _():
        greet({"segment": s - 2})

    @pl.when(p < depth - 1)
    def _():
        greet({"segment": s + 2})

    for k in range(micro):
        x = li_ref[k].astype(jnp.float32)
        inv = lax.rsqrt(jnp.mean(x * x, axis=-1, keepdims=True) + epsilon)
        exact = x * inv
        inv_s[k] = inv
        exact_s[k] = exact
        nrm[0, k, t] = exact.astype(jnp.bfloat16)

    peers = bits + 1 + jnp.minimum(p, 1) + jnp.minimum(depth - 1 - p, 1)
    pl.semaphore_wait(barrier, peers)

    def ag_copy(kind, k, c, m, b):
        buf = (nrm, inc)[kind]
        block = buf.at[0, k, flip(m), piece(c)]
        return copy(k, c, kind, m | 1 << b, block, block, {"tp": flip(1 << b)})

    def ag_arrival(kind, k, c, slot):
        buf = (nrm, inc)[kind]
        block = buf.at[0, k, flip(slot), piece(c)]
        low = slot & -slot
        return copy(k, c, kind, slot, block, block, {"tp": flip(low)})

    def ag_start(kind, k, c):
        for b in reversed(range(bits)):
            ag_copy(kind, k, c, 0, b).start()

    def ag_forward(kind, k):
        for c in range(pieces):
            for m in masks_even(n):
                ag_arrival(kind, k, c, m).wait_recv()
                for b in reversed(range(bits)):
                    if 1 << b < (m & -m):
                        ag_copy(kind, k, c, m, b).start()
                if c == pieces - 1:
                    mirror_copy(kind, k, m).start()

    def ag_finish(kind, k):
        for c in range(pieces):
            for m in range(1, n, 2):
                ag_arrival(kind, k, c, m).wait_recv()

    def mirror_copy(kind, k, m):
        buf = (nrm, inc)[kind]
        block = flip(m)
        return copy(
            k, 0, 3 + kind, m, buf.at[0, k, block], buf.at[1, k, block], {"segment": mirror}
        )

    def pass_copy(kind, k, m, arriving=0):
        block = (nrm, inc)[kind].at[1, k, flip(m | arriving)]
        return copy(k, 0, 5 + kind, m, block, block, {"tp": flip(1)})

    def mirror_pass(kind, k):
        for m in range(0, n, 2):
            mirror_copy(kind, k, m).wait_recv()
            pass_copy(kind, k, m).start()

    def mirror_wait(kind, k):
        for m in range(0, n, 2):
            pass_copy(kind, k, m, 1).wait_recv()

    def forward(side, k):
        start = (side * micro + k) * total
        lhs = nrm[side, k].reshape(total, width)
        step = min(256, hid)

        @pl.loop(0, hid // step)
        def _(j):
            cols = pl.ds(pl.multiple_of(j * step, step), step)
            g = jnp.dot(lhs, gate_w[:, cols], preferred_element_type=jnp.float32)
            u = jnp.dot(lhs, up_w[:, cols], preferred_element_type=jnp.float32)
            sigma = jax.nn.sigmoid(g)
            sl = g * sigma
            hidden_out[start : start + total, cols] = (sl * u).astype(jnp.bfloat16)
            slope[start : start + total, cols] = u * sigma * (1.0 + g * (1.0 - sigma))
            silu_s[start : start + total, cols] = sl

        keep = pl.ds(pl.multiple_of(d * half, half), half)
        normed_out[start : start + total, :] = nrm[side, k, :, :, keep].reshape(total, half)

    def factors(side, k, turned):
        start = (side * micro + k) * total
        lhs = inc[side, k].reshape(total, width)
        step = min(1024, hid)

        @pl.loop(0, hid // step)
        def _(j):
            cols = pl.ds(pl.multiple_of(j * step, step), step)
            if turned:
                grad = jnp.dot(lhs, down_t[:, cols], preferred_element_type=jnp.float32)
            else:
                grad = contract_last(lhs, down_w[cols, :])
            gate_out[start : start + total, cols] = (
                grad * slope[start : start + total, cols]
            ).astype(jnp.bfloat16)
            up_out[start : start + total, cols] = (
                grad * silu_s[start : start + total, cols]
            ).astype(jnp.bfloat16)

    def keep_incoming(side, k):
        start = (side * micro + k) * total
        keep = pl.ds(pl.multiple_of(d * half, half), half)
        incoming_out[start : start + total, :] = inc[side, k, :, :, keep].reshape(total, half)

    def partial_grads(k, turned):
        start = k * total
        step = min(1024, width)

        @pl.loop(0, width // step)
        def _(j):
            gg = gate_out[start : start + total, :]
            ug = up_out[start : start + total, :]
            cols = pl.ds(pl.multiple_of(j * step, step), step)
            if turned:
                part = jnp.dot(gg, gate_t[:, cols], preferred_element_type=jnp.float32)
                part = part + jnp.dot(ug, up_t[:, cols], preferred_element_type=jnp.float32)
            else:
                part = contract_last(gg, gate_w[cols, :]) + contract_last(ug, up_w[cols, :])
            parts[k, :, :, cols] = part.astype(jnp.bfloat16).reshape(n, rows, step)

    def turn(source, target):
        step = 256

        @pl.loop(0, source.shape[1] // step)
        def _(j):
            cols = pl.ds(pl.multiple_of(j * step, step), step)
            target[cols, :] = source[:, cols].T

    def rs_copy(k, c, b, m):
        q = m | 1 << b
        src = parts.at[k, flip(q), piece(c)]
        return copy(k, c, 2, q, src, rs_recv.at[k, q, piece(c)], {"tp": flip(1 << b)})

    def rs_round(k, c, b):
        for m in range(0, n, 1 << (b + 1)):
            q = m | 1 << b
            if b:
                value = parts[k, flip(q), piece(c)].astype(jnp.float32)
                for lower in range(b):
                    value = value + rs_recv[k, q | 1 << lower, piece(c)].astype(jnp.float32)
                parts[k, flip(q), piece(c)] = value.astype(jnp.bfloat16)
            rs_copy(k, c, b, m).start()

    def rs_wait(k, c, b):
        for m in range(0, n, 1 << (b + 1)):
            rs_copy(k, c, b, m).wait_recv()

    def z_copy(k, c, step=2):
        dst = inc.at[0, k, t, piece(c)]
        return copy(k, c, 2, 0, z_send.at[k, piece(c)], dst, {"segment": s + step})

    def finish(k, c):
        span = piece(c)
        value = parts[k, t, span].astype(jnp.float32)
        for b in range(bits):
            value = value + rs_recv[k, 1 << b, span].astype(jnp.float32)
        base = exact_s[k, span]
        back = inc[0, k, t, span].astype(jnp.float32) + inv_s[k, span] * (
            value - base * jnp.mean(value * base, axis=-1, keepdims=True)
        )
        back = back.astype(jnp.bfloat16)
        z_send[k, span] = back

        @pl.when(p < depth - 1)
        def _():
            z_copy(k, c).start()

        back_ref[k, span] = back

    first = p == 0
    early = jnp.logical_and(p > 0, p * 2 >= depth)

    def open_rows(k):
        for c in range(pieces):
            ag_start(0, k, c)

        @pl.when(first)
        def _():
            inc[0, k, t] = cot_ref[d, k]
            for c in range(pieces):
                ag_start(1, k, c)

        mirror_copy(0, k, 0).start()

        @pl.when(first)
        def _():
            mirror_copy(1, k, 0).start()

    def spread(k):
        ag_forward(0, k)

        @pl.when(first)
        def _():
            ag_forward(1, k)

        ag_finish(0, k)

    def mirror_forward():
        for k in range(micro):
            mirror_pass(0, k)
        for k in range(micro):
            mirror_wait(0, k)
            forward(1, k)

    for k in range(micro):
        open_rows(k)
    spread(0)
    loads[0].wait()
    loads[1].wait()
    forward(0, 0)
    loads[2].wait()

    @pl.when(jnp.logical_not(first))
    def _():
        for k in range(1, micro):
            spread(k)
            forward(0, k)
        turn(down_w, down_t)
        turn(gate_w, gate_t)
        turn(up_w, up_t)

    @pl.when(early)
    def _():
        mirror_forward()

    def receive(k):
        @pl.when(jnp.logical_not(first))
        def _():
            for c in range(pieces):
                z_copy(k, c, -2).wait_recv()
                ag_start(1, k, c)
            mirror_copy(1, k, 0).start()

    def relay(k):
        @pl.when(jnp.logical_not(first))
        def _():
            ag_forward(1, k)

    def compute(k):
        ag_finish(1, k)

        @pl.when(first)
        def _():
            factors(0, k, False)
            partial_grads(k, False)

        @pl.when(jnp.logical_not(first))
        def _():
            factors(0, k, True)
            partial_grads(k, True)

        for c in range(pieces):
            rs_round(k, c, 0)
        keep_incoming(0, k)

    def reduce(k):
        for b in range(1, bits):
            for c in range(pieces):
                rs_wait(k, c, b - 1)
                rs_round(k, c, b)

    def end(k):
        for c in range(pieces):
            rs_wait(k, c, bits - 1)
            finish(k, c)

    def mirror_factors(k, turned):
        mirror_wait(1, k)
        factors(1, k, turned)
        keep_incoming(1, k)

    receive(0)
    relay(0)
    compute(0)

    for k in range(1, micro):
        reduce(k - 1)

        @pl.when(first)
        def _():
            spread(k)
            forward(0, k)

        receive(k)
        relay(k)
        end(k - 1)
        mirror_pass(1, k - 1)
        compute(k)
    reduce(micro - 1)
    mirror_pass(1, micro - 1)

    @pl.when(early)
    def _():
        for k in range(micro - 1):
            mirror_factors(k, True)

    @pl.when(jnp.logical_and(early, p == depth - 1))
    def _():
        mirror_factors(micro - 1, True)

    end(micro - 1)

    @pl.when(jnp.logical_and(early, p < depth - 1))
    def _():
        mirror_factors(micro - 1, True)

    @pl.when(jnp.logical_not(early))
    def _():
        mirror_forward()
        for k in range(micro):
            mirror_factors(k, False)

    for k in range(micro):
        for kind in range(2):
            for m in range(0, n, 2):
                mirror_copy(kind, k, m).wait_send()
                pass_copy(kind, k, m).wait_send()
        for c in range(pieces):
            for b in range(bits):
                for m in range(0, n, 1 << (b + 1)):
                    for kind in range(2):
                        ag_copy(kind, k, c, m, b).wait_send()
                    rs_copy(k, c, b, m).wait_send()

            @pl.when(p < depth - 1)
            def _():
                z_copy(k, c).wait_send()


def relayed(
    segments,
    n,
    layer_inputs,
    cotangent,
    gate_weight,
    up_weight,
    down_weight,
    gate_momentum,
    up_momentum,
    down_momentum,
):
    _, micro, rows, width = layer_inputs.shape
    hid = gate_weight.shape[2]
    half = width // 2
    flat = 2 * micro * n * rows
    vmem = pl.BlockSpec(memory_space=pltpu.VMEM)
    hbm = pl.BlockSpec(memory_space=pl.ANY)
    pieces = 2 if rows % 32 == 0 else 1
    bf, f32 = jnp.bfloat16, jnp.float32
    back, normed, incoming, hidden, gate, up = pl.pallas_call(
        functools.partial(relay_kernel, n, segments // 2),
        name="relay",
        out_shape=(
            jax.ShapeDtypeStruct((micro, rows, width), bf),
            jax.ShapeDtypeStruct((flat, half), bf),
            jax.ShapeDtypeStruct((flat, half), bf),
            jax.ShapeDtypeStruct((flat, hid), bf),
            jax.ShapeDtypeStruct((flat, hid), bf),
            jax.ShapeDtypeStruct((flat, hid), bf),
        ),
        in_specs=[vmem, vmem, hbm, hbm, hbm],
        out_specs=(vmem,) * 6,
        scratch_shapes=[
            pltpu.VMEM((width, hid), bf),
            pltpu.VMEM((width, hid), bf),
            pltpu.VMEM((hid, width), bf),
            pltpu.VMEM((2, micro, n, rows, width), bf),
            pltpu.VMEM((2, micro, n, rows, width), bf),
            pltpu.VMEM((flat, hid), f32),
            pltpu.VMEM((flat, hid), f32),
            pltpu.VMEM((micro, rows, width), f32),
            pltpu.VMEM((micro, rows, 1), f32),
            pltpu.VMEM((micro, n, rows, width), bf),
            pltpu.VMEM((micro, n, rows, width), bf),
            pltpu.VMEM((micro, rows, width), bf),
            pltpu.VMEM((hid, width), bf),
            pltpu.VMEM((hid, width), bf),
            pltpu.VMEM((width, hid), bf),
            pltpu.SemaphoreType.DMA((3,)),
            pltpu.SemaphoreType.DMA((micro, pieces, 7 * n)),
            pltpu.SemaphoreType.DMA((micro, pieces, 7 * n)),
        ],
        compiler_params=pltpu.CompilerParams(
            collective_id=0, has_side_effects=True, vmem_limit_bytes=60 << 20
        ),
    )(layer_inputs[0], cotangent, gate_weight[0], up_weight[0], down_weight[0])
    new_gate = momentum_decay * gate_momentum[0] + contract_rows(normed, gate)
    new_up = momentum_decay * up_momentum[0] + contract_rows(normed, up)
    new_down = momentum_decay * down_momentum[0] + contract_rows(hidden, incoming)
    return (back[None], new_gate[None], new_up[None], new_down[None])


def choose(segments, n, *arrays):
    rows = arrays[0].shape[2]
    if rows % 16 == 0 and n > 1 and n & (n - 1) == 0:
        return relayed(segments, n, *arrays)
    return shards(*arrays)


def solution(mesh):
    body = functools.partial(choose, mesh.shape["segment"], mesh.shape["tp"])
    return jax.shard_map(
        body,
        mesh=mesh,
        in_specs=(
            P("segment", None, "tp", None),
            P(None, None, "tp", None),
            P("segment", None, "tp"),
            P("segment", None, "tp"),
            P("segment", "tp", None),
            P("segment", None, "tp"),
            P("segment", None, "tp"),
            P("segment", "tp", None),
        ),
        out_specs=(
            P("segment", None, "tp", None),
            P("segment", None, "tp"),
            P("segment", None, "tp"),
            P("segment", "tp", None),
        ),
        check_vma=False,
    )
```

profile of v0, /device:TPU:24, one launch (start us, length us, event | category | flops | bytes accessed | tf_op | source)
XLA Modules:
  0.0 105.9 jit_solution(14497722159128803658)
XLA Ops:
  0.6 90.9 %relay.1 = (bf16[2,32,2048]{2,1,0:T(8,128)(2,1)}, bf16[512,1024]{1,0:T(8,128)(2,1)}, bf16[512,1024]{1,0:T(8,128)(2,1)}, bf16[512,1024]{1,0:T(8,128)(2,1)}, bf16[...) custom-call(bf16[2,32,2048]{2,1,0:T(8,128)(2,1)} %bitcast.32, bf16[2,2,32,2048]{3,2,1,0:T(8,128)(2,1)} %cot_ref.1, ...), custom_call_target="tpu_custom_call" | custom-call | tf_op jit(solution)/shard_map/relay/pallas_call | solution.py:640
  91.5 0.0 copy-start
  91.5 0.0 copy-start.1
  91.5 0.0 copy-start.5
  91.6 6.3 %fusion.2 = f32[1,1024,1024]{2,1,0:T(8,128)} fusion(f32[1,1024,1024]{2,1,0:T(8,128)} %param.13, bf16[512,1024]{1,0:T(8,128)(2,1)} %get-tuple-element.11, bf16[512,1024]{1,0:T(8,128)(2,1)} %get-tuple-element.12), kind=kOutput, calls=%fused_computation.5 | convolution fusion | flops 1075838976 | bytes 10485760 | tf_op jit(solution)/shard_map/dot_general | solution.py:36
  97.8 0.0 copy-done
  97.8 0.0 copy-done.1
  97.8 0.0 copy-done.5
  97.8 0.0 copy-start.2
  97.9 0.0 copy-start.3
  97.9 0.0 copy-start.4
  97.9 3.4 %fusion.1 = f32[1,1024,1024]{2,1,0:T(8,128)} fusion(f32[1,1024,1024]{2,1,0:T(8,128)S(1)} %copy-done.1, bf16[512,1024]{1,0:T(8,128)(2,1)S(1)} %copy-done, bf16[512,1024]{1,0:T(8,128)(2,1)S(1)} %copy-done.5), kind=kOutput, calls=%fused_computation.3 | convolution fusion | flops 1075838976 | bytes 10485760 | tf_op jit(solution)/shard_map/dot_general | solution.py:36
  101.2 0.0 copy-done.2
  101.2 0.0 copy-done.3
  101.2 0.6 copy-done.4
  101.8 0.0 copy-start.6
  101.8 3.4 %fusion = f32[1,1024,1024]{2,1,0:T(8,128)} fusion(f32[1,1024,1024]{2,1,0:T(8,128)S(1)} %copy-done.2, bf16[512,1024]{1,0:T(8,128)(2,1)S(1)} %copy-done.3, bf16[512,1024]{1,0:T(8,128)(2,1)S(1)} %copy-done.4), kind=kOutput, calls=%fused_computation.1 | convolution fusion | flops 1075838976 | bytes 10485760 | tf_op jit(solution)/shard_map/dot_general | solution.py:36
  105.2 0.0 copy-done.6
  105.2 0.7 copy.13
Async XLA Ops:
  91.5 6.3 %copy-start = (bf16[512,1024]{1,0:T(8,128)(2,1)S(1)}, bf16[512,1024]{1,0:T(8,128)(2,1)}, u32[]{:S(2)}) copy-start(bf16[512,1024]{1,0:T(8,128)(2,1)} %get-tuple-element.11) | copy-start | bytes 3145732
  91.5 6.3 %copy-start.1 = (f32[1,1024,1024]{2,1,0:T(8,128)S(1)}, f32[1,1024,1024]{2,1,0:T(8,128)}, u32[]{:S(2)}) copy-start(f32[1,1024,1024]{2,1,0:T(8,128)} %param.14) | copy-start | bytes 12582916
  91.5 6.3 %copy-start.5 = (bf16[512,1024]{1,0:T(8,128)(2,1)S(1)}, bf16[512,1024]{1,0:T(8,128)(2,1)}, u32[]{:S(2)}) copy-start(bf16[512,1024]{1,0:T(8,128)(2,1)} %get-tuple-element.13) | copy-start | bytes 3145732
  97.8 3.4 %copy-start.2 = (f32[1,1024,1024]{2,1,0:T(8,128)S(1)}, f32[1,1024,1024]{2,1,0:T(8,128)}, u32[]{:S(2)}) copy-start(f32[1,1024,1024]{2,1,0:T(8,128)} %param.15) | copy-start | bytes 12582916
  97.9 3.4 %copy-start.3 = (bf16[512,1024]{1,0:T(8,128)(2,1)S(1)}, bf16[512,1024]{1,0:T(8,128)(2,1)}, u32[]{:S(2)}) copy-start(bf16[512,1024]{1,0:T(8,128)(2,1)} %get-tuple-element.14) | copy-start | bytes 3145732
  97.9 4.0 %copy-start.4 = (bf16[512,1024]{1,0:T(8,128)(2,1)S(1)}, bf16[512,1024]{1,0:T(8,128)(2,1)}, u32[]{:S(2)}) copy-start(bf16[512,1024]{1,0:T(8,128)(2,1)} %get-tuple-element.15) | copy-start | bytes 3145732
  101.8 3.4 %copy-start.6 = (bf16[2,32,2048]{2,1,0:T(8,128)(2,1)S(1)}, bf16[2,32,2048]{2,1,0:T(8,128)(2,1)}, u32[]{:S(2)}) copy-start(bf16[2,32,2048]{2,1,0:T(8,128)(2,1)} %get-tuple-element.10) | copy-start | bytes 786436
where the time goes:
time: 106 us
  Pallas kernels  90.9 us (86%)
  matrix products  13 us (12%)
  local copies, waits for them, and re-layouts  1.32 us (1%)
    pallas_call x1, Pallas kernels, relayed(): pl.pallas_call(functools.partial(relay_kernel, n, segments // 2), name='r...  90.9 us
    dot_general x3, matrix products, contract_rows(): lax.dot_general(left, right, (((0,), (0,)), ((), ())), preferred_element_...  13 us

commit v1 on v0

v1 whole, which is shorter than its diff:
```python
import functools
import jax
import jax.numpy as jnp
from jax import lax
from jax.experimental import pallas as pl
from jax.experimental.pallas import tpu as pltpu
from jax.sharding import PartitionSpec as P

epsilon = 1e-05
momentum_decay = 0.9


def passed_along(block, axis, distance):
    devices = range(lax.axis_size(axis))
    route = [(i - distance, i) for i in devices if i - distance in devices]
    return lax.ppermute(block, axis, route)


def partner(block, axis, distance):
    count = lax.axis_size(axis)
    route = []
    for low in range(count):
        high = low | 1 << distance
        if high != low and high < count:
            route += [(low, high), (high, low)]
    return lax.ppermute(block, axis, route)


def contract_last(left, right):
    return lax.dot_general(
        left, right, (((1,), (1,)), ((), ())), preferred_element_type=jnp.float32
    )


def contract_rows(left, right):
    return lax.dot_general(
        left, right, (((0,), (0,)), ((), ())), preferred_element_type=jnp.float32
    )


def rounded(values):
    return lax.optimization_barrier(values.astype(jnp.bfloat16)).astype(jnp.float32)


def project(rows, gate_w, up_w):
    gate = jnp.dot(rows, gate_w, preferred_element_type=jnp.float32)
    up = jnp.dot(rows, up_w, preferred_element_type=jnp.float32)
    return (gate, up)


def backward_factors(incoming_rows, gate, up, down_w):
    hidden_grad = contract_last(incoming_rows, down_w)
    sigma = jax.nn.sigmoid(gate)
    silu = gate * sigma
    hidden = (silu * up).astype(jnp.bfloat16)
    gate_grad = (hidden_grad * up * sigma * (1.0 + gate * (1.0 - sigma))).astype(jnp.bfloat16)
    up_grad = (hidden_grad * silu).astype(jnp.bfloat16)
    return (hidden, gate_grad, up_grad)


def owned(array, start, size, axis):
    return lax.dynamic_slice_in_dim(array, start, size, axis)


def shards(
    layer_inputs,
    cotangent,
    gate_weight,
    up_weight,
    down_weight,
    gate_momentum,
    up_momentum,
    down_momentum,
):
    segments = lax.axis_size("segment")
    depth = segments // 2
    segment = lax.axis_index("segment")
    direction = segment % 2
    lower = direction == 0
    position = segment // 2
    gate_w = gate_weight[0]
    up_w = up_weight[0]
    down_w = down_weight[0]
    inputs = layer_inputs[0].astype(jnp.float32)
    micro, rows_dev, width = inputs.shape
    half = width // 2
    hidden_dev = gate_w.shape[1]
    total_rows = rows_dev * lax.axis_size("tp")
    inverse_norm = lax.rsqrt(jnp.mean(inputs * inputs, axis=-1, keepdims=True) + epsilon)
    exact = inputs * inverse_norm
    normed = exact.astype(jnp.bfloat16)
    entry = lax.dynamic_index_in_dim(cotangent, direction, 0, keepdims=False)
    ticks = depth + micro - 1
    wide_store = jnp.zeros((micro, total_rows, width), jnp.bfloat16)
    narrow_store = jnp.zeros((micro, total_rows, hidden_dev), jnp.bfloat16)
    extra = (wide_store, narrow_store, narrow_store, narrow_store) + (wide_store,)

    def process(tick, received, state):
        outgoing, backs, extra = state
        index = tick - position
        active = (index >= 0) & (index < micro)
        slot = jnp.clip(index, 0, micro - 1)
        local_in = jnp.where(position == 0, entry[slot], received)
        incoming_rows = lax.all_gather(local_in, "tp", axis=0, tiled=True)
        full_rows = lax.all_gather(normed[slot], "tp", axis=0, tiled=True)

        def factors():
            gate, up = project(full_rows, gate_w, up_w)
            return backward_factors(incoming_rows, gate, up, down_w)

        def resting():
            blank = jnp.zeros((total_rows, hidden_dev), jnp.bfloat16)
            return (blank, blank, blank)

        hidden, gate_grad, up_grad = lax.cond(active, factors, resting)
        count = lax.axis_size("tp") * rows_dev

        def compute():
            return contract_last(gate_grad, gate_w) + contract_last(up_grad, up_w)

        def quiet():
            return jnp.zeros((count, width), jnp.float32)

        normed_grad = lax.psum_scatter(
            lax.cond(active, compute, quiet).astype(jnp.bfloat16),
            "tp",
            scatter_dimension=0,
            tiled=True,
        ).astype(jnp.float32)
        scale = inverse_norm[slot]
        base = exact[slot]
        back = local_in.astype(jnp.float32) + scale * (
            normed_grad - base * jnp.mean(normed_grad * base, axis=-1, keepdims=True)
        )
        back = back.astype(jnp.bfloat16)
        backs = lax.dynamic_update_index_in_dim(
            backs, jnp.where(active, back, backs[slot]), slot, 0
        )
        fresh = (incoming_rows, hidden, gate_grad, up_grad) + (full_rows,)
        extra = tuple(
            (
                lax.dynamic_update_index_in_dim(
                    store, jnp.where(active, item, store[slot]), slot, 0
                )
                for store, item in zip(extra, fresh)
            )
        )
        return (back, backs, extra)

    zero_rows = jnp.zeros((rows_dev, width), jnp.bfloat16)
    state = process(
        0, zero_rows, (zero_rows, jnp.zeros((micro, rows_dev, width), jnp.bfloat16), extra)
    )

    def advance(tick, state):
        received = passed_along(state[0], "segment", 2)
        return process(tick, received, state)

    outgoing, backs, extra = lax.fori_loop(1, ticks, advance, state)
    keep_start = jnp.where(lower, 0, half)
    send_start = half - keep_start
    flat_rows = micro * total_rows
    normed_all = extra[4]
    normed_flat = normed_all.reshape(flat_rows, width)
    incoming_flat = extra[0].reshape(flat_rows, width)
    hidden_flat = extra[1].reshape(flat_rows, hidden_dev)
    gate_flat = extra[2].reshape(flat_rows, hidden_dev)
    up_flat = extra[3].reshape(flat_rows, hidden_dev)
    arrived = partner(
        (
            owned(normed_flat, send_start, half, 1),
            owned(incoming_flat, send_start, half, 1),
            hidden_flat,
            gate_flat,
            up_flat,
        ),
        "segment",
        0,
    )
    normed_keep = owned(normed_flat, keep_start, half, 1)
    incoming_keep = owned(incoming_flat, keep_start, half, 1)
    gate_share = contract_rows(normed_keep, gate_flat) + rounded(
        contract_rows(arrived[0], arrived[3])
    )
    up_share = contract_rows(normed_keep, up_flat) + rounded(contract_rows(arrived[0], arrived[4]))
    down_share = contract_rows(hidden_flat, incoming_keep) + rounded(
        contract_rows(arrived[2], arrived[1])
    )
    new_gate = (momentum_decay * gate_momentum[0] + gate_share)[None]
    new_up = (momentum_decay * up_momentum[0] + up_share)[None]
    new_down = (momentum_decay * down_momentum[0] + down_share)[None]
    return (backs[None], new_gate, new_up, new_down)


CHUNKS = 4
VMEM_LIMIT = 42 << 20
ORDER = (
    ("R00 R01 R02 R03", "F00 F01 K00 F02", "K01 F03 K02 K03"),
    ("E0 P00 S0 P01", "P02 Q00 n1 P03", "Q01 Q02 Q03"),
    ("h10 h11 h12 h13", "N1 R10 R11", "R12 R13"),
    ("G00 G01 G02 G03", "f10 f11 K10 f12", "K11 f13 K12 K13", "E1"),
    ("P10 S1 P11 P12", "Q10 P13 Q11", "Q12 Q13"),
    ("X00 X01 X02 X03", "L0 U0 G10 X10", "G11 X11 G12 X12", "G13 X13"),
    ("V0 l0 u0", "L1 l1"),
)


def scope(name):
    return jax.named_scope(name)


def update(d, k, nrm, inc, hidden, gate_g, up_g, accs, news, scale=False, done=None):
    _, chunks, sides, n, rows, span = nrm.shape
    total = sides * n * rows
    hid = hidden.shape[2]
    keep = d * (chunks // 2)
    step = 256

    def add(which, where, value):
        old = accs[which][where]
        news[which][where] = (old * momentum_decay if scale else old) + value
        if done is not None:
            done(which, where)

    @pl.loop(0, chunks // 2)
    def _(j):
        place = pl.ds(pl.multiple_of(j * span, span), span)
        lhs = nrm[k, keep + j].reshape(total, span)
        rhs = inc[k, keep + j].reshape(total, span)

        @pl.loop(0, hid // step)
        def _(i):
            piece = pl.ds(pl.multiple_of(i * step, step), step)
            add(0, (place, piece), contract_rows(lhs, gate_g[k, :, piece]))
            add(1, (place, piece), contract_rows(lhs, up_g[k, :, piece]))
            add(2, (piece, place), contract_rows(hidden[k, :, piece], rhs))


def apply_kernel(
    back, gate_acc, up_acc, down_acc, nrm, inc, hidden, gate_g, up_g,
    back_out, gate_out, up_out, down_out, gate_new, up_new, down_new, sems,
):
    d = lax.rem(lax.axis_index("segment"), 2)
    accs = (gate_acc, up_acc, down_acc)
    news = (gate_new, up_new, down_new)
    outs = (gate_out, up_out, down_out)
    backs = pltpu.make_async_copy(back, back_out, sems.at[3])
    backs.start()

    def done(which, where):
        pltpu.make_async_copy(
            news[which].at[where], outs[which].at[where], sems.at[which]
        ).start()

    update(d, nrm.shape[0] - 1, nrm, inc, hidden, gate_g, up_g, accs, news, done=done)
    for which in range(3):
        pltpu.make_async_copy(news[which], outs[which], sems.at[which]).wait()
    backs.wait()


def semaphore_keys(micro, chunks, n):
    slots = [1] + list(range(2, n, 2))
    bits = n.bit_length() - 1
    keys = []
    for k in range(micro):
        keys += [("normed", k, m) for m in slots]
        keys += [("mirror", k), ("pass", k)]
        keys += [("sum", k, chunks, b) for b in range(bits)]
        for c in range(chunks):
            keys += [("rows", k, c, m) for m in slots]
            keys += [("sum", k, c, b) for b in range(bits)]
            keys += [("mirror", k, c), ("pass", k, c), ("hop", k, c)]
    return {key: i for i, key in enumerate(keys)}


def relay_kernel(
    n,
    depth,
    li_hbm,
    cot_hbm,
    gate_hbm,
    up_hbm,
    down_hbm,
    gate_m,
    up_m,
    down_m,
    back_ref,
    gate_acc,
    up_acc,
    down_acc,
    nrm,
    inc,
    hidden,
    gate_g,
    up_g,
    gate_w,
    up_w,
    down_w,
    gate_t,
    up_t,
    down_t,
    li_ref,
    cot_ref,
    slope,
    silu_s,
    slant,
    grad_s,
    exact_s,
    inv_s,
    mean_s,
    parts,
    rs_recv,
    stats,
    st_recv,
    z_send,
    load_sem,
    cot_sem,
    ssem,
    rsem,
):
    micro, rows, width = li_ref.shape
    hid = down_w.shape[0]
    chunks, span = nrm.shape[1], nrm.shape[5]
    total = n * rows
    half = width // 2
    bits = n.bit_length() - 1
    s = lax.axis_index("segment")
    t = lax.axis_index("tp")
    p = lax.div(s, 2)
    d = lax.rem(s, 2)
    mirror = s + 1 - 2 * d
    first = p == 0
    early = jnp.logical_and(p > 0, p * 2 >= depth)
    last = p == depth - 1

    def flip(mask):
        value = t
        for b in range(bits):
            if mask >> b & 1:
                value = value + (1 << b) * (1 - 2 * lax.rem(lax.div(t, 1 << b), 2))
        return value

    def cols(c):
        return pl.ds(c * span, span)

    barrier = pltpu.get_barrier_semaphore()

    def greet(device):
        pl.semaphore_signal(
            barrier, inc=1, device_id=device, device_id_type=pl.DeviceIdType.MESH
        )

    for b in range(bits):
        greet({"tp": flip(1 << b)})
    greet({"segment": mirror})

    @pl.when(p > 0)
    def _():
        greet({"segment": s - 2})

    @pl.when(p < depth - 1)
    def _():
        greet({"segment": s + 2})

    sources = (li_hbm, down_hbm, gate_hbm, up_hbm, gate_m, up_m, down_m)
    targets = (li_ref, down_w, gate_w, up_w, gate_acc, up_acc, down_acc)
    loads = [
        pltpu.make_async_copy(a, b, load_sem.at[i])
        for i, (a, b) in enumerate(zip(sources, targets))
    ]

    cot_load = pltpu.make_async_copy(cot_hbm.at[d], cot_ref, cot_sem)
    loads[0].start()
    pl.when(first)(cot_load.start)
    for load in loads[1:4]:
        load.start()

    keys = semaphore_keys(micro, chunks, n)

    def copy(group, key, src, dst, device):
        return pltpu.make_async_remote_copy(
            src_ref=src,
            dst_ref=dst,
            send_sem=ssem.at[group],
            recv_sem=rsem.at[keys[key]],
            device_id=device,
            device_id_type=pl.DeviceIdType.MESH,
        )

    def arrived(key, ref):
        copy(0, key, ref, ref, {"tp": flip(1)}).wait_recv()

    evens = sorted(range(2, n, 2), key=lambda m: -(m & -m))

    def spread(ref, key, m, b):
        block = ref.at[flip(m)]
        slot = m | 1 << b
        copy(0, key + (slot if b else 1,), block, block, {"tp": flip(1 << b)}).start()

    def cross(kind, k, c, m, start=True):
        if kind:
            source, target, key = inc.at[k, c, 0], inc.at[k, c, 1], ("mirror", k, c)
            source, target = source.at[flip(m)], target.at[flip(m)]
        else:
            source, target, key = nrm.at[k, :, 0, flip(m)], nrm.at[k, :, 1, flip(m)], ("mirror", k)
        copy(2, key, source, target, {"segment": mirror}).start()

    def normed_copy(k, m, b):
        block = nrm.at[k, :, 0, flip(m)]
        copy(0, ("normed", k, m | 1 << b if b else 1), block, block, {"tp": flip(1 << b)}).start()

    def normed_start(k):
        for b in reversed(range(bits)):
            normed_copy(k, 0, b)

    def normed_forward(k):
        for m in evens:
            arrived(("normed", k, m), nrm.at[k, :, 0, flip(m)])
            for b in reversed(range(bits)):
                if 1 << b < (m & -m):
                    normed_copy(k, m, b)
            cross(0, k, 0, m)

    def normed_wait(k):
        arrived(("normed", k, 1), nrm.at[k, :, 0, pl.ds(0, n // 2)])

    def rows_start(k, c):
        for b in reversed(range(bits)):
            spread(inc.at[k, c, 0], ("rows", k, c), 0, b)

    def rows_forward(k, c):
        for m in evens:
            arrived(("rows", k, c, m), inc.at[k, c, 0, flip(m)])
            for b in reversed(range(bits)):
                if 1 << b < (m & -m):
                    spread(inc.at[k, c, 0], ("rows", k, c), m, b)
            cross(1, k, c, m)

    def rows_wait(k, c):
        arrived(("rows", k, c, 1), inc.at[k, c, 0, pl.ds(0, n // 2)])

    def normed_pass(k):
        arrived(("mirror", k), nrm.at[k, :, 1, pl.ds(0, n // 2)])
        for m in range(0, n, 2):
            block = nrm.at[k, :, 1, flip(m)]
            copy(2, ("pass", k), block, block, {"tp": flip(1)}).start()

    def rows_pass(k, c):
        arrived(("mirror", k, c), inc.at[k, c, 1, pl.ds(0, n // 2)])
        for m in range(0, n, 2):
            block = inc.at[k, c, 1, flip(m)]
            copy(2, ("pass", k, c), block, block, {"tp": flip(1)}).start()

    def turn(source, target):
        step = 256

        @pl.loop(0, source.shape[1] // step)
        def _(j):
            piece = pl.ds(pl.multiple_of(j * step, step), step)
            target[piece, :] = source[:, piece].T

    def forward(side, k):
        step = min(256, hid)
        here = pl.ds(side * total, total)

        @pl.loop(0, hid // step)
        def _(j):
            piece = pl.ds(pl.multiple_of(j * step, step), step)
            g = jnp.zeros((total, step), jnp.float32)
            u = jnp.zeros((total, step), jnp.float32)
            for c in range(chunks):
                lhs = nrm[k, c, side].reshape(total, span)
                g = g + jnp.dot(lhs, gate_w[cols(c), piece], preferred_element_type=jnp.float32)
                u = u + jnp.dot(lhs, up_w[cols(c), piece], preferred_element_type=jnp.float32)
            sigma = jax.nn.sigmoid(g)
            sl = g * sigma
            sp = u * sigma * (1.0 + g * (1.0 - sigma))
            hidden[k, here, piece] = (sl * u).astype(jnp.bfloat16)
            slope[k, here, piece] = sp
            silu_s[k, here, piece] = sl
            if side == 0:
                slant[k, :, piece] = sp * g + sl * u

    def accumulate(side, k, c):
        lhs = inc[k, c, side].reshape(total, span)
        value = jnp.dot(lhs, down_t[cols(c), :], preferred_element_type=jnp.float32)
        if c:
            value = grad_s[side] + value
        grad_s[side] = value

    def factors(side, k):
        here = pl.ds(side * total, total)
        step = min(128, hid)
        sums = jnp.zeros((total, step), jnp.float32)
        for j in range(hid // step):
            piece = pl.ds(j * step, step)
            grad = grad_s[side, :, piece]
            gate_g[k, here, piece] = (grad * slope[k, here, piece]).astype(jnp.bfloat16)
            up_g[k, here, piece] = (grad * silu_s[k, here, piece]).astype(jnp.bfloat16)
            if side == 0:
                sums = sums + grad * slant[k, :, piece]
        if side == 0:
            stats[k] = sums.reshape(n, rows, step)

    def partial_grads(k, c):
        gg = gate_g[k, :total, :]
        ug = up_g[k, :total, :]
        part = jnp.dot(gg, gate_t[:, cols(c)], preferred_element_type=jnp.float32)
        part = part + jnp.dot(ug, up_t[:, cols(c)], preferred_element_type=jnp.float32)
        parts[k, c] = part.astype(jnp.bfloat16).reshape(n, rows, span)

    def rs_refs(k, c):
        if c == chunks:
            return stats.at[k], st_recv.at[k]
        return parts.at[k, c], rs_recv.at[k, c]

    def rs_round(k, c, b):
        source, target = rs_refs(k, c)
        for m in range(0, n, 1 << (b + 1)):
            q = m | 1 << b
            if b:
                value = source[flip(q)].astype(jnp.float32)
                for lower in range(b):
                    value = value + target[q | 1 << lower].astype(jnp.float32)
                source[flip(q)] = value.astype(source.dtype)
            copy(
                1 if c == chunks else 0,
                ("sum", k, c, b),
                source.at[flip(q)],
                target.at[q],
                {"tp": flip(1 << b)},
            ).start()

    def rs_wait(k, c, b):
        arrived(("sum", k, c, b), rs_refs(k, c)[1].at[pl.ds(0, n >> (b + 1))])

    def rs_total(k, c):
        source, target = rs_refs(k, c)
        value = source[t].astype(jnp.float32)
        for b in range(bits):
            value = value + target[1 << b].astype(jnp.float32)
        return value

    def receive(k, c):
        @pl.when(jnp.logical_not(first))
        def _():
            arrived(("hop", k, c), inc.at[k, c, 0, t])
            rows_start(k, c)
            cross(1, k, c, 0)

    def reduce(k, c):
        for b in range(1, bits):
            rs_wait(k, c, b - 1)
            rs_round(k, c, b)

    def finish(k, c):
        if c == 0:
            rs_wait(k, chunks, bits - 1)
            sums = rs_total(k, chunks)
            mean_s[k] = jnp.sum(sums, axis=-1, keepdims=True) * (1.0 / width)
        rs_wait(k, c, bits - 1)
        value = rs_total(k, c)
        own = inc[k, c, 0, t].astype(jnp.float32)
        back = own + inv_s[k] * (value - exact_s[k, c] * mean_s[k])
        back = back.astype(jnp.bfloat16)
        z_send[k, c] = back

        @pl.when(p < depth - 1)
        def _():
            target = inc.at[k, c, 0, t]
            copy(3, ("hop", k, c), z_send.at[k, c], target, {"segment": s + 2}).start()

        back_ref[k, :, cols(c)] = back

    loads[0].wait()
    for k in range(micro):
        x = li_ref[k].astype(jnp.float32)
        inv = lax.rsqrt(jnp.mean(x * x, axis=-1, keepdims=True) + epsilon)
        inv_s[k] = inv
        for c in range(chunks):
            exact = x[:, c * span : (c + 1) * span] * inv
            exact_s[k, c] = exact
            nrm[k, c, 0, t] = exact.astype(jnp.bfloat16)

    @pl.when(first)
    def _():
        cot_load.wait()
        for k in range(micro):
            for c in range(chunks):
                inc[k, c, 0, t] = cot_ref[k, :, cols(c)]

    peers = bits + 1 + jnp.minimum(p, 1) + jnp.minimum(depth - 1 - p, 1)
    with scope("barrier"):
        pl.semaphore_wait(barrier, peers)

    normed_start(0)
    for k in range(micro):
        cross(0, k, 0, 0)

    def mirror_forward():
        for k in range(micro):
            normed_pass(k)
        for k in range(micro):
            arrived(("pass", k), nrm.at[k, :, 1, pl.ds(0, n // 2)])
            forward(1, k)

    def cot_start(k):
        @pl.when(first)
        def _():
            for c in range(chunks):
                rows_start(k, c)
            for c in range(chunks):
                cross(1, k, c, 0)

    with scope("t1"):
        loads[1].wait()
        turn(down_w, down_t)
    cot_start(0)
    with scope("t2"):
        loads[2].wait()
        loads[3].wait()
        for load in loads[4:]:
            load.start()
        turn(gate_w, gate_t)
    for k in range(1, micro):
        normed_start(k)
    with scope("nf0"):
        pl.when(jnp.logical_not(first))(lambda: normed_forward(0))
    with scope("t3"):
        turn(up_w, up_t)
    for k in range(1, micro):
        cot_start(k)
    with scope("nf0f"):
        pl.when(first)(lambda: normed_forward(0))
    with scope("nw0"):
        normed_wait(0)
    with scope("fw0"):
        forward(0, 0)

    def later():
        for k in range(1, micro):
            normed_forward(k)
            normed_wait(k)
            forward(0, k)

    with scope("fw1"):
        pl.when(jnp.logical_not(first))(later)
    with scope("mf"):
        pl.when(early)(mirror_forward)

    def op_R(k, c):
        receive(k, c)

    def op_F(k, c):
        rows_forward(k, c)

    def op_f(k, c):
        pl.when(jnp.logical_not(first))(lambda: rows_forward(k, c))

    def op_h(k, c):
        pl.when(first)(lambda: rows_forward(k, c))

    def op_n(k):
        pl.when(first)(lambda: normed_forward(k))

    def op_N(k):
        def run():
            normed_wait(k)
            forward(0, k)

        pl.when(first)(run)

    def op_K(k, c):
        rows_wait(k, c)
        accumulate(0, k, c)

    def op_E(k):
        factors(0, k)
        rs_round(k, chunks, 0)

    def op_P(k, c):
        partial_grads(k, c)
        rs_round(k, c, 0)

    def op_S(k):
        reduce(k, chunks)

    def op_Q(k, c):
        reduce(k, c)

    def op_G(k, c):
        finish(k, c)

    def op_X(k, c):
        rows_pass(k, c)

    def op_M(k):
        for c in range(chunks):
            arrived(("pass", k, c), inc.at[k, c, 1, pl.ds(0, n // 2)])
            accumulate(1, k, c)
        factors(1, k)

    def op_A(k):
        if k == 0:
            for load in loads[4:]:
                load.wait()
        accs = (gate_acc, up_acc, down_acc)
        update(d, k, nrm, inc, hidden, gate_g, up_g, accs, accs, scale=k == 0)

    def op_L(k):
        pl.when(early)(lambda: op_M(k))

    def op_U(k):
        pl.when(last)(lambda: op_A(k))

    def op_V(k):
        pl.when(jnp.logical_not(early))(mirror_forward)

    def op_l(k):
        pl.when(jnp.logical_not(early))(lambda: op_M(k))

    def op_u(k):
        pl.when(jnp.logical_not(last))(lambda: op_A(k))

    ops = dict(
        R=op_R, F=op_F, f=op_f, h=op_h, N=op_N, n=op_n, K=op_K, E=op_E, P=op_P, S=op_S,
        Q=op_Q, G=op_G, X=op_X, M=op_M, A=op_A, L=op_L, U=op_U, V=op_V, l=op_l, u=op_u,
    )
    for name in [x for line in ORDER for part in line for x in part.split()]:
        with scope(name):
            ops[name[0]](*(int(x) for x in name[1:]))

    block = rows * span
    sizes = (
        micro * chunks * (n - 1) * 3 * block,
        micro * (n - 1) * rows * 128,
        micro * chunks * 2 * n * block,
        micro * chunks * block,
    )

    def sends_done(group, ref):
        view = ref.at[pl.ds(0, sizes[group] // ref.shape[1])]
        copy(group, ("normed", 0, 1), view, view, {"tp": flip(1)}).wait_send()

    with scope("sends"):
        sends_done(0, gate_w)
        sends_done(1, gate_acc)
        sends_done(2, gate_w)
        pl.when(p < depth - 1)(lambda: sends_done(3, gate_w))


def relayed(
    segments,
    n,
    layer_inputs,
    cotangent,
    gate_weight,
    up_weight,
    down_weight,
    gate_momentum,
    up_momentum,
    down_momentum,
):
    _, micro, rows, width = layer_inputs.shape
    hid = gate_weight.shape[2]
    half = width // 2
    chunks = CHUNKS
    span = width // chunks
    total = n * rows
    hbm = pl.BlockSpec(memory_space=pl.ANY)
    bf, f32 = jnp.bfloat16, jnp.float32
    ends = pl.pallas_call(
        functools.partial(relay_kernel, n, segments // 2),
        name="relay",
        out_shape=(
            pltpu.VMEM((micro, rows, width), bf),
            pltpu.VMEM((half, hid), f32),
            pltpu.VMEM((half, hid), f32),
            pltpu.VMEM((hid, half), f32),
            pltpu.VMEM((micro, chunks, 2, n, rows, span), bf),
            pltpu.VMEM((micro, chunks, 2, n, rows, span), bf),
            pltpu.VMEM((micro, 2 * total, hid), bf),
            pltpu.VMEM((micro, 2 * total, hid), bf),
            pltpu.VMEM((micro, 2 * total, hid), bf),
        ),
        in_specs=[hbm] * 8,
        scratch_shapes=[
            pltpu.VMEM((width, hid), bf),
            pltpu.VMEM((width, hid), bf),
            pltpu.VMEM((hid, width), bf),
            pltpu.VMEM((hid, width), bf),
            pltpu.VMEM((hid, width), bf),
            pltpu.VMEM((width, hid), bf),
            pltpu.VMEM((micro, rows, width), bf),
            pltpu.VMEM((micro, rows, width), bf),
            pltpu.VMEM((micro, 2 * total, hid), f32),
            pltpu.VMEM((micro, 2 * total, hid), f32),
            pltpu.VMEM((micro, total, hid), f32),
            pltpu.VMEM((2, total, hid), f32),
            pltpu.VMEM((micro, chunks, rows, span), f32),
            pltpu.VMEM((micro, rows, 1), f32),
            pltpu.VMEM((micro, rows, 1), f32),
            pltpu.VMEM((micro, chunks, n, rows, span), bf),
            pltpu.VMEM((micro, chunks, n, rows, span), bf),
            pltpu.VMEM((micro, n, rows, 128), f32),
            pltpu.VMEM((micro, n, rows, 128), f32),
            pltpu.VMEM((micro, chunks, rows, span), bf),
            pltpu.SemaphoreType.DMA((7,)),
            pltpu.SemaphoreType.DMA(()),
            pltpu.SemaphoreType.DMA((4,)),
            pltpu.SemaphoreType.DMA((len(semaphore_keys(micro, chunks, n)),)),
        ],
        compiler_params=pltpu.CompilerParams(
            collective_id=0, has_side_effects=True, vmem_limit_bytes=VMEM_LIMIT
        ),
    )(
        layer_inputs[0],
        cotangent,
        gate_weight[0],
        up_weight[0],
        down_weight[0],
        gate_momentum[0],
        up_momentum[0],
        down_momentum[0],
    )
    vmem = pl.BlockSpec(memory_space=pltpu.VMEM)
    back, new_gate, new_up, new_down = pl.pallas_call(
        apply_kernel,
        name="apply",
        out_shape=(
            jax.ShapeDtypeStruct((micro, rows, width), bf),
            jax.ShapeDtypeStruct((half, hid), f32),
            jax.ShapeDtypeStruct((half, hid), f32),
            jax.ShapeDtypeStruct((hid, half), f32),
        ),
        in_specs=[vmem] * 9,
        out_specs=(hbm,) * 4,
        scratch_shapes=[
            pltpu.VMEM((half, hid), f32),
            pltpu.VMEM((half, hid), f32),
            pltpu.VMEM((hid, half), f32),
            pltpu.SemaphoreType.DMA((4,)),
        ],
        compiler_params=pltpu.CompilerParams(vmem_limit_bytes=13 << 20),
    )(*ends)
    return (back[None], new_gate[None], new_up[None], new_down[None])


def choose(segments, n, *arrays):
    rows = arrays[0].shape[2]
    if rows % 16 == 0 and n > 1 and n & (n - 1) == 0 and segments > 2:
        return relayed(segments, n, *arrays)
    return shards(*arrays)


def solution(mesh):
    body = functools.partial(choose, mesh.shape["segment"], mesh.shape["tp"])
    return jax.shard_map(
        body,
        mesh=mesh,
        in_specs=(
            P("segment", None, "tp", None),
            P(None, None, "tp", None),
            P("segment", None, "tp"),
            P("segment", None, "tp"),
            P("segment", "tp", None),
            P("segment", None, "tp"),
            P("segment", None, "tp"),
            P("segment", "tp", None),
        ),
        out_specs=(
            P("segment", None, "tp", None),
            P("segment", None, "tp"),
            P("segment", None, "tp"),
            P("segment", "tp", None),
        ),
        check_vma=False,
    )
```

time: 106 us -> 85.6 us (0.81)
  matrix products: 13 us -> 0 us
  Pallas kernels: 90.9 us -> 84.5 us
  local copies, waits for them, and re-layouts: 1.32 us -> 0 us
    dot_general x3 -> x0, matrix products: 13 us -> none  [contract_rows(): lax.dot_general(left, right, (((0,), (0,)), ((), ())), preferred_element_...]
    pallas_call x1, Pallas kernels: 90.9 us -> 79.5 us  [relayed(): pl.pallas_call(functools.partial(relay_kernel, n, segments // 2), name='r...]
    pallas_call x0 -> x1, Pallas kernels: none -> 4.96 us  [relayed(): pl.pallas_call(apply_kernel, name='apply', out_shape=(jax.ShapeDtypeStruc...]
    unnamed x15 -> x0, local copies, waits for them, and re-layouts: 1.32 us -> none
where the time goes in v1:
time: 85.6 us; the launch traced here: 85.1 us
  Pallas kernels  84.5 us (99%)
    pallas_call x1, Pallas kernels, relayed(): pl.pallas_call(functools.partial(relay_kernel, n, segments // 2), name='r...  79.5 us
    pallas_call x1, Pallas kernels, relayed(): pl.pallas_call(apply_kernel, name='apply', out_shape=(jax.ShapeDtypeStruc...  4.96 us

profile of v1, /device:TPU:24, one launch (start us, length us, event | category | flops | bytes accessed | tf_op | source)
XLA Modules:
  0.0 85.1 jit_solution(562220757342944336)
XLA Ops:
  0.6 79.5 %relay.1 = (bf16[2,32,2048]{2,1,0:T(8,128)(2,1)S(1)}, f32[1024,1024]{1,0:T(8,128)S(1)}, f32[1024,1024]{1,0:T(8,128)S(1)}, f32[1024,1024]{1,0:T(8,128)S(1)}, bf16...) custom-call(bf16[2,32,2048]{2,1,0:T(8,128)(2,1)} %bitcast.17, ...), custom_call_target="tpu_custom_call" | custom-call | tf_op jit(solution)/shard_map/relay/pallas_call | solution.py:772
  80.1 5.0 %apply.1 = (bf16[2,32,2048]{2,1,0:T(8,128)(2,1)}, f32[1024,1024]{1,0:T(8,128)}, f32[1024,1024]{1,0:T(8,128)}, f32[1024,1024]{1,0:T(8,128)}) custom-call(bf16[2,32,2048]{2,1,0:T(8,128)(2,1)S(1)} %get-tuple-element.17.back, f32[1024,1024]{1,0:T(8,128)S(1)} %get-tuple-element.18.gate_acc, f32[1024,1024]{1,0:T(8,128)S(1)} %get-tuple-element.19.up_acc, ...), custom_call_target="tpu_custom_call" | custom-call | tf_op jit(solution)/shard_map/apply/pallas_call | solution.py:827

commit v2 on v1

--- a/solution.py
+++ b/solution.py
@@ -194,51 +194,49 @@
 
 CHUNKS = 4
 VMEM_LIMIT = 42 << 20
-ORDER = (
-    ("R00 R01 R02 R03", "F00 F01 K00 F02", "K01 F03 K02 K03"),
-    ("E0 P00 S0 P01", "P02 Q00 n1 P03", "Q01 Q02 Q03"),
-    ("h10 h11 h12 h13", "N1 R10 R11", "R12 R13"),
-    ("G00 G01 G02 G03", "f10 f11 K10 f12", "K11 f13 K12 K13", "E1"),
-    ("P10 S1 P11 P12", "Q10 P13 Q11", "Q12 Q13"),
-    ("X00 X01 X02 X03", "L0 U0 G10 X10", "G11 X11 G12 X12", "G13 X13"),
-    ("V0 l0 u0", "L1 l1"),
-)
 
 
 def scope(name):
     return jax.named_scope(name)
 
 
-def update(d, k, nrm, inc, hidden, gate_g, up_g, accs, news, scale=False, done=None):
+def update(d, plan, nrm, inc, hidden, gate_g, up_g, flipped, accs, news, done=None):
     _, chunks, sides, n, rows, span = nrm.shape
     total = sides * n * rows
     hid = hidden.shape[2]
     keep = d * (chunks // 2)
     step = 256
 
-    def add(which, where, value):
-        old = accs[which][where]
-        news[which][where] = (old * momentum_decay if scale else old) + value
-        if done is not None:
-            done(which, where)
-
     @pl.loop(0, chunks // 2)
     def _(j):
         place = pl.ds(pl.multiple_of(j * span, span), span)
-        lhs = nrm[k, keep + j].reshape(total, span)
-        rhs = inc[k, keep + j].reshape(total, span)
+        flipped[...] = nrm[plan[0][1][0], keep + j].reshape(total, span).T
 
         @pl.loop(0, hid // step)
         def _(i):
             piece = pl.ds(pl.multiple_of(i * step, step), step)
-            add(0, (place, piece), contract_rows(lhs, gate_g[k, :, piece]))
-            add(1, (place, piece), contract_rows(lhs, up_g[k, :, piece]))
-            add(2, (piece, place), contract_rows(hidden[k, :, piece], rhs))
+            for which, ks, scale in plan:
+                where = (piece, place) if which == 2 else (place, piece)
+                value = accs[which][where]
+                if scale:
+                    value = value * momentum_decay
+                for k in ks:
+                    if which == 2:
+                        rhs = inc[k, keep + j].reshape(total, span)
+                        value = value + contract_rows(hidden[k, :, piece], rhs)
+                    else:
+                        grads = (gate_g, up_g)[which][k, :, piece]
+                        value = value + jnp.dot(
+                            flipped[...], grads, preferred_element_type=jnp.float32
+                        )
+                news[which][where] = value
+                if done is not None:
+                    done(which, where)
 
 
 def apply_kernel(
     back, gate_acc, up_acc, down_acc, nrm, inc, hidden, gate_g, up_g,
-    back_out, gate_out, up_out, down_out, gate_new, up_new, down_new, sems,
+    back_out, gate_out, up_out, down_out, gate_new, up_new, down_new, flipped, sems,
 ):
     d = lax.rem(lax.axis_index("segment"), 2)
     accs = (gate_acc, up_acc, down_acc)
@@ -252,7 +250,9 @@
             news[which].at[where], outs[which].at[where], sems.at[which]
         ).start()
 
-    update(d, nrm.shape[0] - 1, nrm, inc, hidden, gate_g, up_g, accs, news, done=done)
+    final = nrm.shape[0] - 1
+    plan = ((0, (final,), False), (1, (final,), False), (2, range(final + 1), True))
+    update(d, plan, nrm, inc, hidden, gate_g, up_g, flipped, accs, news, done=done)
     for which in range(3):
         pltpu.make_async_copy(news[which], outs[which], sems.at[which]).wait()
     backs.wait()
@@ -270,6 +270,7 @@
             keys += [("rows", k, c, m) for m in slots]
             keys += [("sum", k, c, b) for b in range(bits)]
             keys += [("mirror", k, c), ("pass", k, c), ("hop", k, c)]
+            keys += [("side", k, c)] if k else []
     return {key: i for i, key in enumerate(keys)}
 
 
@@ -313,6 +314,8 @@
     stats,
     st_recv,
     z_send,
+    z_side,
+    flipped,
     load_sem,
     cot_sem,
     ssem,
@@ -324,6 +327,7 @@
     total = n * rows
     half = width // 2
     bits = n.bit_length() - 1
+    top = n // 2
     s = lax.axis_index("segment")
     t = lax.axis_index("tp")
     p = lax.div(s, 2)
@@ -370,10 +374,13 @@
     ]
 
     cot_load = pltpu.make_async_copy(cot_hbm.at[d], cot_ref, cot_sem)
+    def start_weights():
+        for load in loads[1:4]:
+            load.start()
+
     loads[0].start()
     pl.when(first)(cot_load.start)
-    for load in loads[1:4]:
-        load.start()
+    pl.when(jnp.logical_not(first))(start_weights)
 
     keys = semaphore_keys(micro, chunks, n)
 
@@ -459,7 +466,7 @@
             piece = pl.ds(pl.multiple_of(j * step, step), step)
             target[piece, :] = source[:, piece].T
 
-    def forward(side, k):
+    def forward(side, k, also=False):
         step = min(256, hid)
         here = pl.ds(side * total, total)
 
@@ -480,6 +487,8 @@
             silu_s[k, here, piece] = sl
             if side == 0:
                 slant[k, :, piece] = sp * g + sl * u
+            if also:
+                up_t[piece, :] = up_w[:, piece].T
 
     def accumulate(side, k, c):
         lhs = inc[k, c, side].reshape(total, span)
@@ -542,11 +551,21 @@
         return value
 
     def receive(k, c):
-        @pl.when(jnp.logical_not(first))
+        arrived(("hop", k, c), inc.at[k, c, 0, t])
+        if k == 0:
+            rows_start(k, c)
+        else:
+            for b in range(bits - 1):
+                spread(inc.at[k, c, 0], ("rows", k, c), 0, b)
+        cross(1, k, c, 0)
+
+    def detour(k, c):
+        @pl.when(p < depth - 1)
         def _():
-            arrived(("hop", k, c), inc.at[k, c, 0, t])
-            rows_start(k, c)
-            cross(1, k, c, 0)
+            arrived(("side", k, c), z_side.at[k - 1, c])
+            target = inc.at[k, c, 0, flip(top)]
+            device = {"segment": s + 2}
+            copy(4, ("rows", k, c, top), z_side.at[k - 1, c], target, device).start()
 
     def reduce(k, c):
         for b in range(1, bits):
@@ -569,10 +588,19 @@
         def _():
             target = inc.at[k, c, 0, t]
             copy(3, ("hop", k, c), z_send.at[k, c], target, {"segment": s + 2}).start()
+            if k:
+                target = z_side.at[k - 1, c]
+                copy(4, ("side", k, c), z_send.at[k, c], target, {"tp": flip(top)}).start()
 
         back_ref[k, :, cols(c)] = back
 
     loads[0].wait()
+
+    @pl.when(first)
+    def _():
+        cot_load.wait()
+        start_weights()
+
     for k in range(micro):
         x = li_ref[k].astype(jnp.float32)
         inv = lax.rsqrt(jnp.mean(x * x, axis=-1, keepdims=True) + epsilon)
@@ -584,7 +612,6 @@
 
     @pl.when(first)
     def _():
-        cot_load.wait()
         for k in range(micro):
             for c in range(chunks):
                 inc[k, c, 0, t] = cot_ref[k, :, cols(c)]
@@ -624,111 +651,149 @@
         turn(gate_w, gate_t)
     for k in range(1, micro):
         normed_start(k)
-    with scope("nf0"):
-        pl.when(jnp.logical_not(first))(lambda: normed_forward(0))
-    with scope("t3"):
-        turn(up_w, up_t)
     for k in range(1, micro):
         cot_start(k)
-    with scope("nf0f"):
-        pl.when(first)(lambda: normed_forward(0))
+    with scope("nf0"):
+        normed_forward(0)
     with scope("nw0"):
         normed_wait(0)
     with scope("fw0"):
-        forward(0, 0)
-
-    def later():
+        forward(0, 0, True)
+
+    def project_all():
         for k in range(1, micro):
             normed_forward(k)
             normed_wait(k)
             forward(0, k)
 
     with scope("fw1"):
-        pl.when(jnp.logical_not(first))(later)
+        pl.when(jnp.logical_not(first))(project_all)
     with scope("mf"):
         pl.when(early)(mirror_forward)
 
-    def op_R(k, c):
-        receive(k, c)
-
-    def op_F(k, c):
-        rows_forward(k, c)
-
-    def op_f(k, c):
-        pl.when(jnp.logical_not(first))(lambda: rows_forward(k, c))
-
-    def op_h(k, c):
-        pl.when(first)(lambda: rows_forward(k, c))
-
-    def op_n(k):
-        pl.when(first)(lambda: normed_forward(k))
-
-    def op_N(k):
-        def run():
-            normed_wait(k)
-            forward(0, k)
-
-        pl.when(first)(run)
-
-    def op_K(k, c):
+    def side_gather(k, c):
+        arrived(("pass", k, c), inc.at[k, c, 1, pl.ds(0, n // 2)])
+        accumulate(1, k, c)
+
+    def gather(k, c):
         rows_wait(k, c)
         accumulate(0, k, c)
 
-    def op_E(k):
+    def factor(k):
         factors(0, k)
         rs_round(k, chunks, 0)
 
-    def op_P(k, c):
+    def partial(k, c):
         partial_grads(k, c)
         rs_round(k, c, 0)
 
-    def op_S(k):
-        reduce(k, chunks)
-
-    def op_Q(k, c):
-        reduce(k, c)
-
-    def op_G(k, c):
-        finish(k, c)
-
-    def op_X(k, c):
-        rows_pass(k, c)
-
-    def op_M(k):
-        for c in range(chunks):
-            arrived(("pass", k, c), inc.at[k, c, 1, pl.ds(0, n // 2)])
-            accumulate(1, k, c)
-        factors(1, k)
-
-    def op_A(k):
+    def change(k):
         if k == 0:
             for load in loads[4:]:
                 load.wait()
         accs = (gate_acc, up_acc, down_acc)
-        update(d, k, nrm, inc, hidden, gate_g, up_g, accs, accs, scale=k == 0)
-
-    def op_L(k):
-        pl.when(early)(lambda: op_M(k))
-
-    def op_U(k):
-        pl.when(last)(lambda: op_A(k))
-
-    def op_V(k):
+        plan = ((0, (k,), k == 0), (1, (k,), k == 0))
+        update(d, plan, nrm, inc, hidden, gate_g, up_g, flipped, accs, accs)
+
+    def project(k):
+        normed_wait(k)
+        forward(0, k)
+
+    def mirrored():
         pl.when(jnp.logical_not(early))(mirror_forward)
 
-    def op_l(k):
-        pl.when(jnp.logical_not(early))(lambda: op_M(k))
-
-    def op_u(k):
-        pl.when(jnp.logical_not(last))(lambda: op_A(k))
-
-    ops = dict(
-        R=op_R, F=op_F, f=op_f, h=op_h, N=op_N, n=op_n, K=op_K, E=op_E, P=op_P, S=op_S,
-        Q=op_Q, G=op_G, X=op_X, M=op_M, A=op_A, L=op_L, U=op_U, V=op_V, l=op_l, u=op_u,
-    )
-    for name in [x for line in ORDER for part in line for x in part.split()]:
-        with scope(name):
-            ops[name[0]](*(int(x) for x in name[1:]))
+    def traced(name, step):
+        return step
+
+    R, F, K = traced("R", receive), traced("F", rows_forward), traced("K", gather)
+    E, P = traced("E", factor), traced("P", partial)
+    S, Q = traced("S", lambda k: reduce(k, chunks)), traced("Q", reduce)
+    G, H, X = traced("G", finish), traced("H", detour), traced("X", rows_pass)
+    N, W, V = traced("N", normed_forward), traced("W", project), traced("V", mirrored)
+    m, M = traced("m", side_gather), traced("M", lambda k: factors(1, k))
+    U = traced("U", change)
+
+    def each(*pairs):
+        for c in range(chunks):
+            for step, k in pairs:
+                step(k, c)
+
+    def products(k, between=None, fill=None):
+        for c in range(chunks):
+            if c == 2:
+                S(k)
+            P(k, c)
+            if c >= 2:
+                Q(k, c - 2)
+                if fill is not None:
+                    fill(k - 1, c - 2)
+        if between is not None:
+            between(1)
+        for c in range(chunks - 2, chunks):
+            Q(k, c)
+            if fill is not None:
+                fill(k - 1, c)
+
+    def finals():
+        each((X, 0))
+        each((G, 1))
+        each((H, 1))
+        each((X, 1))
+        V()
+        each((m, 0))
+        M(0)
+        U(0)
+        each((m, 1))
+        M(1)
+
+    def play_first():
+        each((F, 0))
+        each((K, 0))
+        E(0)
+        products(0, between=N)
+        each((F, 1))
+        W(1)
+        each((G, 0), (K, 1))
+        E(1)
+        products(1)
+        finals()
+
+    def play_middle():
+        each((R, 0))
+        each((F, 0))
+        each((K, 0))
+        E(0)
+        products(0)
+        each((R, 1))
+        each((F, 1), (G, 0))
+        each((K, 1))
+        E(1)
+        products(1)
+        finals()
+
+    def play_last():
+        each((R, 0))
+        each((F, 0))
+        each((K, 0))
+        E(0)
+        products(0)
+        each((R, 1))
+        each((X, 0))
+        each((F, 1))
+        each((K, 1))
+        E(1)
+        products(1, fill=m)
+        M(0)
+        each((X, 1))
+        each((G, 0))
+        U(0)
+        each((m, 1))
+        M(1)
+        each((G, 1))
+
+    pl.when(first)(play_first)
+    pl.when(jnp.logical_not(jnp.logical_or(first, last)))(play_middle)
+    pl.when(last)(play_last)
 
     block = rows * span
     sizes = (
@@ -736,17 +801,24 @@
         micro * (n - 1) * rows * 128,
         micro * chunks * 2 * n * block,
         micro * chunks * block,
+        2 * (micro - 1) * chunks * block,
+        micro * chunks * (n - 1) * 3 * block - (micro - 1) * chunks * block,
     )
 
-    def sends_done(group, ref):
-        view = ref.at[pl.ds(0, sizes[group] // ref.shape[1])]
+    def sends_done(group, ref, size=None):
+        view = ref.at[pl.ds(0, sizes[group if size is None else size] // ref.shape[1])]
         copy(group, ("normed", 0, 1), view, view, {"tp": flip(1)}).wait_send()
 
     with scope("sends"):
-        sends_done(0, gate_w)
+        pl.when(first)(lambda: sends_done(0, gate_w))
+        pl.when(jnp.logical_not(first))(lambda: sends_done(0, gate_w, 5))
         sends_done(1, gate_acc)
         sends_done(2, gate_w)
-        pl.when(p < depth - 1)(lambda: sends_done(3, gate_w))
+
+        @pl.when(p < depth - 1)
+        def _():
+            sends_done(3, gate_w)
+            sends_done(4, gate_w)
 
 
 def relayed(
@@ -805,9 +877,11 @@
             pltpu.VMEM((micro, n, rows, 128), f32),
             pltpu.VMEM((micro, n, rows, 128), f32),
             pltpu.VMEM((micro, chunks, rows, span), bf),
+            pltpu.VMEM((micro - 1, chunks, rows, span), bf),
+            pltpu.VMEM((span, 2 * total), bf),
             pltpu.SemaphoreType.DMA((7,)),
             pltpu.SemaphoreType.DMA(()),
-            pltpu.SemaphoreType.DMA((4,)),
+            pltpu.SemaphoreType.DMA((5,)),
             pltpu.SemaphoreType.DMA((len(semaphore_keys(micro, chunks, n)),)),
         ],
         compiler_params=pltpu.CompilerParams(
@@ -839,6 +913,7 @@
             pltpu.VMEM((half, hid), f32),
             pltpu.VMEM((half, hid), f32),
             pltpu.VMEM((hid, half), f32),
+            pltpu.VMEM((span, 2 * total), bf),
             pltpu.SemaphoreType.DMA((4,)),
         ],
         compiler_params=pltpu.CompilerParams(vmem_limit_bytes=13 << 20),
@@ -848,7 +923,7 @@
 
 def choose(segments, n, *arrays):
     rows = arrays[0].shape[2]
-    if rows % 16 == 0 and n > 1 and n & (n - 1) == 0 and segments > 2:
+    if rows % 16 == 0 and n == 4 and segments > 2 and arrays[0].shape[1] == 2:
         return relayed(segments, n, *arrays)
     return shards(*arrays)
 

time: 85.6 us -> 76.3 us (0.89)
  Pallas kernels: 84.5 us -> 75 us
    pallas_call x1, Pallas kernels: 79.5 us -> 70 us  [relayed(): pl.pallas_call(functools.partial(relay_kernel, n, segments // 2), name='r...]
where the time goes in v2:
time: 76.3 us; the launch traced here: 75.9 us
  Pallas kernels  75 us (98%)
  between operations  0.82 us (1%)
    pallas_call x1, Pallas kernels, relayed(): pl.pallas_call(functools.partial(relay_kernel, n, segments // 2), name='r...  70 us
    pallas_call x1, Pallas kernels, relayed(): pl.pallas_call(apply_kernel, name='apply', out_shape=(jax.ShapeDtypeStruc...  5.02 us

profile of v2, /device:TPU:24, one launch (start us, length us, event | category | flops | bytes accessed | tf_op | source)
XLA Modules:
  0.0 75.9 jit_solution(2498629818496625975)
XLA Ops:
  0.6 70.0 %relay.1 = (bf16[2,32,2048]{2,1,0:T(8,128)(2,1)S(1)}, f32[1024,1024]{1,0:T(8,128)S(1)}, f32[1024,1024]{1,0:T(8,128)S(1)}, f32[1024,1024]{1,0:T(8,128)S(1)}, bf16...) custom-call(bf16[2,32,2048]{2,1,0:T(8,128)(2,1)} %bitcast.17, ...), custom_call_target="tpu_custom_call" | custom-call | tf_op jit(solution)/shard_map/relay/pallas_call | solution.py:844
  70.7 5.0 %apply.1 = (bf16[2,32,2048]{2,1,0:T(8,128)(2,1)}, f32[1024,1024]{1,0:T(8,128)}, f32[1024,1024]{1,0:T(8,128)}, f32[1024,1024]{1,0:T(8,128)}) custom-call(bf16[2,32,2048]{2,1,0:T(8,128)(2,1)S(1)} %get-tuple-element.17.back, f32[1024,1024]{1,0:T(8,128)S(1)} %get-tuple-element.18.gate_acc, f32[1024,1024]{1,0:T(8,128)S(1)} %get-tuple-element.19.up_acc, ...), custom_call_target="tpu_custom_call" | custom-call | tf_op jit(solution)/shard_map/apply/pallas_call | solution.py:901

commit v3 on v2

--- a/solution.py
+++ b/solution.py
@@ -380,7 +380,7 @@
 
     loads[0].start()
     pl.when(first)(cot_load.start)
-    pl.when(jnp.logical_not(first))(start_weights)
+    start_weights()
 
     keys = semaphore_keys(micro, chunks, n)
 
@@ -595,12 +595,6 @@
         back_ref[k, :, cols(c)] = back
 
     loads[0].wait()
-
-    @pl.when(first)
-    def _():
-        cot_load.wait()
-        start_weights()
-
     for k in range(micro):
         x = li_ref[k].astype(jnp.float32)
         inv = lax.rsqrt(jnp.mean(x * x, axis=-1, keepdims=True) + epsilon)
@@ -610,12 +604,6 @@
             exact_s[k, c] = exact
             nrm[k, c, 0, t] = exact.astype(jnp.bfloat16)
 
-    @pl.when(first)
-    def _():
-        for k in range(micro):
-            for c in range(chunks):
-                inc[k, c, 0, t] = cot_ref[k, :, cols(c)]
-
     peers = bits + 1 + jnp.minimum(p, 1) + jnp.minimum(depth - 1 - p, 1)
     with scope("barrier"):
         pl.semaphore_wait(barrier, peers)
@@ -642,6 +630,14 @@
     with scope("t1"):
         loads[1].wait()
         turn(down_w, down_t)
+
+    @pl.when(first)
+    def _():
+        cot_load.wait()
+        for k in range(micro):
+            for c in range(chunks):
+                inc[k, c, 0, t] = cot_ref[k, :, cols(c)]
+
     cot_start(0)
     with scope("t2"):
         loads[2].wait()
@@ -777,15 +773,20 @@
         each((K, 0))
         E(0)
         products(0)
+        each((X, 0))
         each((R, 1))
-        each((X, 0))
-        each((F, 1))
+        for c in range(chunks - 1):
+            m(0, c)
+        for c in range(chunks):
+            if c == chunks - 2:
+                m(0, chunks - 1)
+            if c == chunks - 1:
+                M(0)
+            F(1, c)
         each((K, 1))
         E(1)
-        products(1, fill=m)
-        M(0)
+        products(1, fill=G)
         each((X, 1))
-        each((G, 0))
         U(0)
         each((m, 1))
         M(1)

time: 76.3 us -> 74.8 us (0.980)
  Pallas kernels: 75 us -> 73.8 us
    pallas_call x1, Pallas kernels: 70 us -> 68.8 us  [relayed(): pl.pallas_call(functools.partial(relay_kernel, n, segments // 2), name='r...]
where the time goes in v3:
time: 74.8 us; the launch traced here: 74.6 us
  Pallas kernels  73.8 us (99%)
  between operations  0.82 us (1%)
    pallas_call x1, Pallas kernels, relayed(): pl.pallas_call(functools.partial(relay_kernel, n, segments // 2), name='r...  68.8 us
    pallas_call x1, Pallas kernels, relayed(): pl.pallas_call(apply_kernel, name='apply', out_shape=(jax.ShapeDtypeStruc...  5.02 us

profile of v3, /device:TPU:24, one launch (start us, length us, event | category | flops | bytes accessed | tf_op | source)
XLA Modules:
  0.0 74.6 jit_solution(10639410776480457191)
XLA Ops:
  0.6 68.8 %relay.1 = (bf16[2,32,2048]{2,1,0:T(8,128)(2,1)S(1)}, f32[1024,1024]{1,0:T(8,128)S(1)}, f32[1024,1024]{1,0:T(8,128)S(1)}, f32[1024,1024]{1,0:T(8,128)S(1)}, bf16...) custom-call(bf16[2,32,2048]{2,1,0:T(8,128)(2,1)} %bitcast.17, ...), custom_call_target="tpu_custom_call" | custom-call | tf_op jit(solution)/shard_map/relay/pallas_call | solution.py:845
  69.4 5.0 %apply.1 = (bf16[2,32,2048]{2,1,0:T(8,128)(2,1)}, f32[1024,1024]{1,0:T(8,128)}, f32[1024,1024]{1,0:T(8,128)}, f32[1024,1024]{1,0:T(8,128)}) custom-call(bf16[2,32,2048]{2,1,0:T(8,128)(2,1)S(1)} %get-tuple-element.17.back, f32[1024,1024]{1,0:T(8,128)S(1)} %get-tuple-element.18.gate_acc, f32[1024,1024]{1,0:T(8,128)S(1)} %get-tuple-element.19.up_acc, ...), custom_call_target="tpu_custom_call" | custom-call | tf_op jit(solution)/shard_map/apply/pallas_call | solution.py:902
